TPU v7x, 32 devices: a whole 2x2x4 slice. The times are simulated.
32 devices in a mesh: gx: 8 (over z, y), gy: 4 (over x, core).
Axes of the slice: x: 2, y: 2, z: 4, core: 2. Of those that a mesh axis runs over, the one named last changes fastest.
Arguments:
- cotangent: float32 [2, 128, 1536], P(None, 'gx', 'gy'), may hold values from -12 to 12
- velocity_in: bfloat16 [2, 128, 1536], P(None, 'gx', 'gy'), may hold values from -6 to 6
- hidden_pre1: bfloat16 [64, 128, 1536], P(None, 'gx', 'gy'), may hold values from -6 to 6
- hidden_pre2: bfloat16 [64, 128, 1536], P(None, 'gx', 'gy'), may hold values from -6 to 6
- w_first: bfloat16 [9, 64, 2], replicated, may hold values from -1.5 to 1.5
- w_middle: bfloat16 [9, 64, 64], replicated, may hold values from -0.25 to 0.25
- w_last: bfloat16 [9, 2, 64], replicated, may hold values from -0.25 to 0.25
Outputs:
- grad_velocity: float32 [2, 128, 1536], P(None, 'gx', 'gy')
- grad_first: float32 [9, 64, 2], replicated
- grad_middle: float32 [9, 64, 64], replicated
- grad_last: float32 [9, 2, 64], replicated
- grad_bias1: float32 [64], replicated
- grad_bias2: float32 [64], replicated
All inputs are finite; a program needn't handle non-finite values.
Results may differ from a plain program's by a relative error of at most 0.0075.
Values may be sent and summed in bfloat16 or wider, within the bound.
A program may use at most 64 MiB of HBM per device.

v0:
```python
import math
import jax
import jax.numpy as jnp
from jax import lax
from jax.sharding import PartitionSpec as P

ITERS = 4
OFFSETS = ((-1, -1), (-1, 0), (-1, 1), (0, -1), (0, 0), (0, 1), (1, -1), (1, 0), (1, 1))


def with_halo(shard, sides, width):
    for axis, dim in sides:
        count, length = (lax.axis_size(axis), shard.shape[dim])
        up = [(i, (i + 1) % count) for i in range(count)]
        down = [(j, i) for i, j in up]
        last = lax.slice_in_dim(shard, length - width, length, axis=dim)
        leading = lax.slice_in_dim(shard, 0, width, axis=dim)
        before = lax.ppermute(last, axis, up)
        after = lax.ppermute(leading, axis, down)
        shard = jnp.concatenate([before, shard, after], axis=dim)
    return shard


def gelu_slope(pre):
    values = pre.astype(jnp.float32)
    _, pullback = jax.vjp(lambda inner: jax.nn.gelu(inner, approximate=True), values)
    return pullback(jnp.ones_like(values))[0]


def window(padded, row_step, col_step, rows, cols):
    return padded[:, 1 + row_step : 1 + row_step + rows, 1 + col_step : 1 + col_step + cols]


def channel_border(field):
    return with_halo(field, (("gx", 1), ("gy", 2)), 1)


def stencil_apply(field):
    padded = with_halo(field, (("gx", 0), ("gy", 1)), 2)
    beside = padded[:-4, 2:-2] + padded[4:, 2:-2] + padded[2:-2, :-4]
    beside = beside + padded[2:-2, 4:]
    return (padded, field - 0.25 * beside)


def paired_sums(residual, image):
    return lax.psum((jnp.sum(residual * residual), jnp.sum(residual * image)), ("gx", "gy"))


def conv_back(weights, padded, rows, cols):
    channels = padded.shape[0]
    total = jnp.zeros((weights.shape[2], rows * cols), jnp.float32)
    for index, (row_step, col_step) in enumerate(OFFSETS):
        shifted = window(padded, -row_step, -col_step, rows, cols).reshape(channels, -1)
        total = total + lax.dot_general(
            weights[index], shifted, (((0,), (0,)), ((), ())), preferred_element_type=jnp.float32
        )
    return total.reshape(weights.shape[2], rows, cols)


def grads_from_padded_deltas(delta_pad, inputs, rows, cols):
    flat_inputs = inputs.reshape(inputs.shape[0], -1)
    results = []
    for row_step, col_step in OFFSETS:
        shifted = window(delta_pad, -row_step, -col_step, rows, cols).reshape(
            delta_pad.shape[0], -1
        )
        results.append(
            lax.dot_general(
                shifted, flat_inputs, (((1,), (1,)), ((), ())), preferred_element_type=jnp.float32
            )
        )
    return jnp.stack(results)


def per_device(cotangent, velocity_in, hidden_pre1, hidden_pre2, w_first, w_middle, w_last):
    rows = cotangent.shape[1]
    cols = cotangent.shape[2]
    factor = 1.0 / math.sqrt(rows * lax.axis_size("gx") * cols * lax.axis_size("gy"))
    hidden1 = jax.nn.gelu(hidden_pre1.astype(jnp.float32), approximate=True).astype(jnp.bfloat16)
    hidden2 = jax.nn.gelu(hidden_pre2.astype(jnp.float32), approximate=True).astype(jnp.bfloat16)
    slope1 = gelu_slope(hidden_pre1)
    slope2 = gelu_slope(hidden_pre2)
    cot_pad = with_halo(cotangent, (("gx", 1), ("gy", 2)), 1)
    along_rows = cot_pad[0, 2:, 1:-1] - cot_pad[0, :-2, 1:-1]
    along_cols = cot_pad[1, 1:-1, 2:] - cot_pad[1, 1:-1, :-2]
    rhs = -0.5 * (along_rows + along_cols)
    lam_pad = jnp.zeros((rows + 4, cols + 4), jnp.float32)
    residual = rhs
    resid_pad, image = stencil_apply(residual)
    norm_now, product = paired_sums(residual, image)
    alpha = norm_now / product
    dir_pad = resid_pad
    along = image
    for step in range(ITERS):
        lam_pad = lam_pad + alpha * dir_pad
        if step + 1 < ITERS:
            residual = residual - alpha * along
            resid_pad, image = stencil_apply(residual)
            norm_next, product = paired_sums(residual, image)
            ratio = norm_next / norm_now
            alpha = norm_next / (product - ratio * norm_next / alpha)
            dir_pad = resid_pad + ratio * dir_pad
            along = image + ratio * along
            norm_now = norm_next
    adjoint_rows = 0.5 * (lam_pad[0 : rows + 2, 1 : cols + 3] - lam_pad[2 : rows + 4, 1 : cols + 3])
    adjoint_cols = 0.5 * (lam_pad[1 : rows + 3, 0 : cols + 2] - lam_pad[1 : rows + 3, 2 : cols + 4])
    adjoint_pad = cot_pad + jnp.stack([adjoint_rows, adjoint_cols])
    adjoint_b = adjoint_pad.astype(jnp.bfloat16)
    delta2 = (conv_back(w_last, adjoint_b, rows, cols) * slope2).astype(jnp.bfloat16)
    delta2_pad = channel_border(delta2)
    delta1 = (conv_back(w_middle, delta2_pad, rows, cols) * slope1).astype(jnp.bfloat16)
    grad_last = grads_from_padded_deltas(adjoint_b, hidden2, rows, cols)
    grad_middle = grads_from_padded_deltas(delta2_pad, hidden1, rows, cols)
    delta1_pad = channel_border(delta1)
    spread = conv_back(w_first, delta1_pad, rows, cols)
    grad_first = grads_from_padded_deltas(delta1_pad, velocity_in, rows, cols)
    grad_velocity = adjoint_pad[:, 1:-1, 1:-1] + spread
    bias_one = jnp.sum(delta1.astype(jnp.float32), axis=(1, 2))
    bias_two = jnp.sum(delta2.astype(jnp.float32), axis=(1, 2))
    summed = lax.psum((grad_first, grad_middle, grad_last, bias_one, bias_two), ("gx", "gy"))
    return (
        grad_velocity,
        factor * summed[0],
        factor * summed[1],
        factor * summed[2],
        factor * summed[3],
        factor * summed[4],
    )


def solution(mesh):
    return jax.shard_map(
        per_device,
        mesh=mesh,
        in_specs=(
            P(None, "gx", "gy"),
            P(None, "gx", "gy"),
            P(None, "gx", "gy"),
            P(None, "gx", "gy"),
            P(),
            P(),
            P(),
        ),
        out_specs=(P(None, "gx", "gy"), P(), P(), P(), P(), P()),
        check_vma=False,
    )
```

profile of v0, /device:TPU:8, one launch (start us, length us, event | category | flops | bytes accessed | tf_op | source)
XLA Modules:
  0.0 423.0 jit_solution(12630795308313707400)
XLA Ops:
  7.2 0.8 fusion.194
  8.0 1.5 collective-permute-start
  9.5 1.4 collective-permute-start.1
  10.9 1.6 collective-permute-done
  13.1 0.8 pad_maximum_fusion.50
  14.5 1.0 collective-permute-done.3
  15.5 2.0 collective-permute-done.2
  17.5 0.9 fusion.98
  18.5 2.5 collective-permute-start.4
  21.4 1.6 collective-permute-done.4
  23.0 1.5 collective-permute-done.5
  24.6 1.7 collective-permute-start.7
  26.3 1.4 collective-permute-done.6
  28.4 42.3 %all-reduce.4 = (f32[]{:T(128)}, f32[]{:T(128)}) all-reduce(f32[]{:T(128)} %get-tuple-element.25, f32[]{:T(128)} %get-tuple-element.24), channel_id=1, replica_groups=mesh['gx'=8,'gy'=4] {'gx','gy'}, use_global_device_ids=true, to_apply=%region_1.0 | all-reduce | flops 2 | bytes 16 | tf_op jit(solution)/shard_map/psum | solution.py:46
  72.1 2.5 collective-permute-start.8
  75.0 1.6 collective-permute-done.8
  76.6 1.6 collective-permute-done.9
  78.3 1.7 collective-permute-start.11
  80.0 1.4 collective-permute-done.10
  82.1 41.4 %all-reduce.3 = (f32[]{:T(128)}, f32[]{:T(128)}) all-reduce(f32[]{:T(128)} %get-tuple-element.23, f32[]{:T(128)} %get-tuple-element.22), channel_id=1, replica_groups=mesh['gx'=8,'gy'=4] {'gx','gy'}, use_global_device_ids=true, to_apply=%region_5.0 | all-reduce | flops 2 | bytes 16 | tf_op jit(solution)/shard_map/psum | solution.py:46
  128.3 2.5 collective-permute-start.12
  131.2 1.6 collective-permute-done.12
  132.8 1.6 collective-permute-done.13
  134.4 1.7 collective-permute-start.15
  136.2 1.4 collective-permute-done.14
  138.3 41.7 %all-reduce.2 = (f32[]{:T(128)}, f32[]{:T(128)}) all-reduce(f32[]{:T(128)} %get-tuple-element.21, f32[]{:T(128)} %get-tuple-element.20), channel_id=1, replica_groups=mesh['gx'=8,'gy'=4] {'gx','gy'}, use_global_device_ids=true, to_apply=%region_9.0 | all-reduce | flops 2 | bytes 16 | tf_op jit(solution)/shard_map/psum | solution.py:46
  184.1 2.5 collective-permute-start.16
  187.1 1.6 collective-permute-done.16
  188.6 1.6 collective-permute-done.17
  190.3 1.7 collective-permute-start.19
  192.0 0.9 pad_maximum_fusion.8
  194.1 41.4 %all-reduce.1 = (f32[]{:T(128)}, f32[]{:T(128)}) all-reduce(f32[]{:T(128)} %get-tuple-element.19, f32[]{:T(128)} %get-tuple-element.18), channel_id=1, replica_groups=mesh['gx'=8,'gy'=4] {'gx','gy'}, use_global_device_ids=true, to_apply=%region_13.0 | all-reduce | flops 2 | bytes 16 | tf_op jit(solution)/shard_map/psum | solution.py:46
  244.7 1.4 convert_reduce_fusion
  249.2 2.5 collective-permute-start.20
  252.6 1.6 collective-permute-done.20
  254.2 1.6 collective-permute-done.21
  256.0 1.7 collective-permute-start.22
  258.1 5.7 %collective-permute-done.23 = bf16[64,18,1]{2,0,1:T(8,128)(2,1)S(1)} collective-permute-done((bf16[64,18,1]{2,0,1:T(8,128)(2,1)S(1)}, bf16[64,18,1]{2,0,1:T(8,128)(2,1)S(1)}, u32[]{:S(2)}, u32[]{:S(2)}) %collective-permute-start.23) | collective-permute-done | bytes 2336 | tf_op jit(solution)/shard_map/ppermute | solution.py:18
  264.0 0.8 maximum_maximum_fusion
  264.8 0.9 fusion.28
  265.8 1.2 slice_bitcast_fusion.6
  266.9 0.8 fusion.21
  267.8 0.8 fusion.27
  268.6 0.9 fusion.26
  269.6 0.8 fusion.25
  270.4 0.8 fusion.24
  271.3 0.9 fusion.23
  277.3 1.2 convert_reduce_fusion.1
  278.6 2.7 collective-permute-start.24
  281.8 0.8 fusion.20
  282.6 0.8 fusion.22
  284.2 1.0 copy.80
  286.0 1.4 collective-permute-start.26
  287.5 1.0 copy.83
  288.6 1.0 copy.77
  289.5 2.7 collective-permute-done.27
  292.2 2.7 collective-permute-done.26
  294.9 0.8 maximum_maximum_fusion.1
  295.7 0.8 slice_bitcast_fusion.1
  296.9 1.6 slice_bitcast_fusion
  301.3 43.5 %all-reduce = (f32[9,64,2]{1,2,0:T(2,128)S(1)}, f32[9,2,64]{2,1,0:T(2,128)S(1)}, f32[64]{0:T(128)S(1)}, f32[64]{0:T(128)S(1)}) all-reduce(f32[9,64,2]{1,2,0:T(2,128)S(1)} %fusion.40, f32[9,2,64]{2,1,0:T(2,128)S(1)} %fusion.31, f32[64]{0:T(128)S(1)} %get-tuple-element.40, ...), channel_id=1, replica_groups=mesh['gx'=8,'gy'=4] {'gx','gy'}, use_global_device_ids=true, to_apply=%region_16.0 | all-reduce | flops 2432 | bytes 19456 | tf_op jit(solution)/shard_map/psum | solution.py:120
  346.5 1.3 copy.84
  352.6 61.8 %all-reduce.7.cloned.1.call-done = f32[9,64,64]{2,1,0:T(8,128)} async-done(((f32[9,64,64]{2,1,0:T(8,128)}), f32[9,64,64]{2,1,0:T(8,128)}) %all-reduce.7.cloned.1.call-update) | async-done | bytes 147472 | tf_op jit(solution)/shard_map/psum | solution.py:120
  414.4 1.7 broadcast_multiply_fusion
  (141 shorter events, 33.6 us)
Async XLA Ops:
  7.2 289.4 %copy-start = (bf16[2,16,384]{2,1,0:T(8,128)(2,1)S(1)}, bf16[2,16,384]{2,1,0:T(8,128)(2,1)}, u32[]{:S(2)}) copy-start(bf16[2,16,384]{2,1,0:T(8,128)(2,1)} %param.8) | copy-start | bytes 73732
  7.2 233.1 %copy-start.11 = (bf16[9,2,64]{2,1,0:T(2,128)(2,1)S(1)}, bf16[9,2,64]{2,1,0:T(2,128)(2,1)}, u32[]{:S(2)}) copy-start(bf16[9,2,64]{2,1,0:T(2,128)(2,1)} %param.13) | copy-start | bytes 6916
  7.2 407.2 %all-reduce.7.cloned.1.call-start = ((), (), s32[]{:S(2)}) async-start(), calls=%async_computation | async-start | bytes 589824 | tf_op jit(solution)/shard_map/psum | solution.py:120
  8.0 4.5 %collective-permute-start = (f32[2,1,384]{2,1,0:T(1,128)S(1)}, f32[2,1,384]{2,1,0:T(1,128)S(1)}, u32[]{:S(2)}, u32[]{:S(2)}) collective-permute-start(f32[2,1,384]{2,1,0:T(1,128)S(1)} %get-tuple-element.78), channel_id=1, source_target_pairs={{0,4},{4,8},{8,12},{12,16},{16,20},{20,24},{24,28},{28,0},{1,5},{5... | collective-permute-start | bytes 9224 | tf_op jit(solution)/shard_map/ppermute | solution.py:18
  9.5 3.6 collective-permute-start.1
  13.9 1.6 collective-permute-start.3
  14.0 3.5 collective-permute-start.2
  18.5 4.5 %collective-permute-start.4 = (f32[2,384]{1,0:T(2,128)S(1)}, f32[2,384]{1,0:T(2,128)S(1)}, u32[]{:S(2)}, u32[]{:S(2)}) collective-permute-start(f32[2,384]{1,0:T(2,128)S(1)} %get-tuple-element.103), channel_id=1, source_target_pairs={{0,4},{4,8},{8,12},{12,16},{16,20},{20,24},{24,28},{28,0},{1,5},{5... | collective-permute-start | bytes 9224 | tf_op jit(solution)/shard_map/ppermute | solution.py:18
  20.9 3.6 collective-permute-start.5
  24.6 3.1 collective-permute-start.6
  24.6 3.1 collective-permute-start.7
  72.1 4.5 %collective-permute-start.8 = (f32[2,384]{1,0:T(2,128)S(1)}, f32[2,384]{1,0:T(2,128)S(1)}, u32[]{:S(2)}, u32[]{:S(2)}) collective-permute-start(f32[2,384]{1,0:T(2,128)S(1)} %get-tuple-element.101), channel_id=1, source_target_pairs={{0,4},{4,8},{8,12},{12,16},{16,20},{20,24},{24,28},{28,0},{1,5},{5... | collective-permute-start | bytes 9224 | tf_op jit(solution)/shard_map/ppermute | solution.py:18
  74.6 3.6 collective-permute-start.9
  78.3 3.1 collective-permute-start.10
  78.3 3.1 collective-permute-start.11
  128.3 4.5 %collective-permute-start.12 = (f32[2,384]{1,0:T(2,128)S(1)}, f32[2,384]{1,0:T(2,128)S(1)}, u32[]{:S(2)}, u32[]{:S(2)}) collective-permute-start(f32[2,384]{1,0:T(2,128)S(1)} %get-tuple-element.99), channel_id=1, source_target_pairs={{0,4},{4,8},{8,12},{12,16},{16,20},{20,24},{24,28},{28,0},{1,5},{5... | collective-permute-start | bytes 9224 | tf_op jit(solution)/shard_map/ppermute | solution.py:18
  130.8 3.6 collective-permute-start.13
  134.4 3.1 collective-permute-start.14
  134.4 3.1 collective-permute-start.15
  184.1 4.5 %collective-permute-start.16 = (f32[2,384]{1,0:T(2,128)S(1)}, f32[2,384]{1,0:T(2,128)S(1)}, u32[]{:S(2)}, u32[]{:S(2)}) collective-permute-start(f32[2,384]{1,0:T(2,128)S(1)} %get-tuple-element.97), channel_id=1, source_target_pairs={{0,4},{4,8},{8,12},{12,16},{16,20},{20,24},{24,28},{28,0},{1,5},{5... | collective-permute-start | bytes 9224 | tf_op jit(solution)/shard_map/ppermute | solution.py:18
  186.6 3.6 collective-permute-start.17
  190.3 3.1 collective-permute-start.18
  190.3 3.1 collective-permute-start.19
  243.6 1.1 copy-start.6
  249.2 5.0 %collective-permute-start.20 = (bf16[64,1,384]{2,0,1:T(8,128)(2,1)S(1)}, bf16[64,1,384]{2,0,1:T(8,128)(2,1)S(1)}, u32[]{:S(2)}, u32[]{:S(2)}) collective-permute-start(bf16[64,1,384]{2,0,1:T(8,128)(2,1)S(1)} %get-tuple-element.72), channel_id=1, source_target_pairs={{0,4},{4,8},{8,12},{12,16},{16,20},{20,24},{24,28},{28,0},{1,5},{5... | collective-permute-start | bytes 147464 | tf_op jit(solution)/shard_map/ppermute | solution.py:18
  251.7 4.1 collective-permute-start.21
  256.0 7.8 %collective-permute-start.23 = (bf16[64,18,1]{2,0,1:T(8,128)(2,1)S(1)}, bf16[64,18,1]{2,0,1:T(8,128)(2,1)S(1)}, u32[]{:S(2)}, u32[]{:S(2)}) collective-permute-start(bf16[64,18,1]{2,0,1:T(8,128)(2,1)S(1)} %get-tuple-element.63), channel_id=1, source_target_pairs={{0,1},{1,2},{2,3},{3,0},{4,5},{5,6},{6,7},{7,4},{8,9},{9,10},{10,1... | collective-permute-start | bytes 6920 | tf_op jit(solution)/shard_map/ppermute | solution.py:18
  256.0 8.0 %collective-permute-start.22 = (bf16[64,18,1]{2,0,1:T(8,128)(2,1)S(1)}, bf16[64,18,1]{2,0,1:T(8,128)(2,1)S(1)}, u32[]{:S(2)}, u32[]{:S(2)}) collective-permute-start(bf16[64,18,1]{2,0,1:T(8,128)(2,1)S(1)} %get-tuple-element.64), channel_id=1, source_target_pairs={{1,0},{2,1},{3,2},{0,3},{5,4},{6,5},{7,6},{4,7},{9,8},{10,9},{11,1... | collective-permute-start | bytes 6920 | tf_op jit(solution)/shard_map/ppermute | solution.py:19
  258.1 6.7 %copy-start.7 = (bf16[64,16,384]{2,1,0:T(8,128)(2,1)S(1)}, bf16[64,16,384]{2,1,0:T(8,128)(2,1)}, u32[]{:S(2)}) copy-start(bf16[64,16,384]{2,1,0:T(8,128)(2,1)} %param.9) | copy-start | bytes 2359300
  272.6 0.9 copy-start.9
  278.6 6.6 %collective-permute-start.24 = (bf16[64,1,384]{2,0,1:T(8,128)(2,1)S(1)}, bf16[64,1,384]{2,0,1:T(8,128)(2,1)S(1)}, u32[]{:S(2)}, u32[]{:S(2)}) collective-permute-start(bf16[64,1,384]{2,0,1:T(8,128)(2,1)S(1)} %get-tuple-element.68), channel_id=1, source_target_pairs={{0,4},{4,8},{8,12},{12,16},{16,20},{20,24},{24,28},{28,0},{1,5},{5... | collective-permute-start | bytes 147464 | tf_op jit(solution)/shard_map/ppermute | solution.py:18
  281.3 4.2 collective-permute-start.25
  283.4 0.7 copy-start.8
  285.6 6.6 %collective-permute-start.27 = (bf16[64,18,1]{2,0,1:T(8,128)(2,1)S(1)}, bf16[64,18,1]{2,0,1:T(8,128)(2,1)S(1)}, u32[]{:S(2)}, u32[]{:S(2)}) collective-permute-start(bf16[64,18,1]{2,0,1:T(8,128)(2,1)S(1)} %get-tuple-element.59), channel_id=1, source_target_pairs={{0,1},{1,2},{2,3},{3,0},{4,5},{5,6},{6,7},{7,4},{8,9},{9,10},{10,1... | collective-permute-start | bytes 6920 | tf_op jit(solution)/shard_map/ppermute | solution.py:18
  286.0 8.9 %collective-permute-start.26 = (bf16[64,18,1]{2,0,1:T(8,128)(2,1)S(1)}, bf16[64,18,1]{2,0,1:T(8,128)(2,1)S(1)}, u32[]{:S(2)}, u32[]{:S(2)}) collective-permute-start(bf16[64,18,1]{2,0,1:T(8,128)(2,1)S(1)} %get-tuple-element.60), channel_id=1, source_target_pairs={{1,0},{2,1},{3,2},{0,3},{5,4},{6,5},{7,6},{4,7},{9,8},{10,9},{11,1... | collective-permute-start | bytes 6920 | tf_op jit(solution)/shard_map/ppermute | solution.py:19
  300.9 46.8 %copy-start.2 = (bf16[16,8,8,384]{3,2,1,0:T(8,128)(2,1)S(1)}, bf16[16,8,8,384]{3,2,1,0:T(8,128)(2,1)}, u32[]{:S(2)}) copy-start(bf16[16,8,8,384]{3,2,1,0:T(8,128)(2,1)} %get-tuple-element.46) | copy-start | bytes 2359300
  346.5 1.4 copy-start.1
  348.1 0.7 copy-start.10
  348.2 1.1 copy-start.5
  348.8 1.2 copy-start.3
  349.8 1.2 copy-start.4
Sparse Core Ops, SparseCore 0:
  284.3 130.0 all-reduce.6
where the time goes:
time: 424 us; the launch traced here: 423 us
  blocking collectives  210 us (50%)
  waiting for transfers between devices  98.9 us (23%)
  starting transfers between devices  32.2 us (8%)
  between operations  28.6 us (7%)
  matrix products  23.7 us (6%)
  other arithmetic  15.2 us (4%)
  local copies, waits for them, and re-layouts  14.1 us (3%)
    psum x4, blocking collectives, paired_sums(): lax.psum((jnp.sum(residual * residual), jnp.sum(residual * image)), ('gx'...  167 us
    psum x1, waiting for transfers between devices, per_device(): lax.psum((grad_first, grad_middle, grad_last, bias_one, bias_two), ('gx',...  61.8 us
    psum x1, blocking collectives, per_device(): lax.psum((grad_first, grad_middle, grad_last, bias_one, bias_two), ('gx',...  43.5 us
    ppermute x14, waiting for transfers between devices, with_halo(): before = lax.ppermute(last, axis, up)  24.5 us
    ppermute x14, starting transfers between devices, with_halo(): before = lax.ppermute(last, axis, up)  17.7 us
    ppermute x14, starting transfers between devices, with_halo(): after = lax.ppermute(leading, axis, down)  14.4 us
    dot_general x27, matrix products, grads_from_padded_deltas(): lax.dot_general(shifted, flat_inputs, (((1,), (1,)), ((), ())), preferred...  14.4 us
    ppermute x14, waiting for transfers between devices, with_halo(): after = lax.ppermute(leading, axis, down)  12.6 us
  transfers between devices with their start and end apart: 29, of which 24 were waited for; matrix products, arithmetic and copies ran while one was open for 5% of the time, Pallas kernels for 0%

commit v1 on v0

--- a/solution.py
+++ b/solution.py
@@ -6,6 +6,11 @@
 
 ITERS = 4
 OFFSETS = ((-1, -1), (-1, 0), (-1, 1), (0, -1), (0, 0), (0, 1), (1, -1), (1, 0), (1, 1))
+
+
+def one_after_other(x, one, other):
+    half = lax.psum(x, one)
+    return lax.psum(half, other)
 
 
 def with_halo(shard, sides, width):
@@ -117,7 +122,7 @@
     grad_velocity = adjoint_pad[:, 1:-1, 1:-1] + spread
     bias_one = jnp.sum(delta1.astype(jnp.float32), axis=(1, 2))
     bias_two = jnp.sum(delta2.astype(jnp.float32), axis=(1, 2))
-    summed = lax.psum((grad_first, grad_middle, grad_last, bias_one, bias_two), ("gx", "gy"))
+    summed = one_after_other((grad_first, grad_middle, grad_last, bias_one, bias_two), "gy", "gx")
     return (
         grad_velocity,
         factor * summed[0],

time: 424 us -> 441 us (1.040)
  waiting for transfers between devices: 98.9 us -> 107 us
  blocking collectives: 210 us -> 217 us
    psum x1 -> x2, waiting for transfers between devices: 61.8 us -> 68.8 us  [the longest x1 68.8 us: one_after_other(): return lax.psum(half, other)]
    psum x1 -> x2, blocking collectives: 43.5 us -> 50 us  [the longest x1 37.1 us: one_after_other(): return lax.psum(half, other)]
  transfers between devices with their start and end apart: 29 -> 30, of which waited for: 24 -> 24; matrix products, arithmetic and copies ran while one was open for 5% -> 4% of each run, Pallas kernels for 0% -> 0%
where the time goes in v1:
time: 441 us; the launch traced here: 437 us
  blocking collectives  217 us (49%)
  waiting for transfers between devices  107 us (24%)
  starting transfers between devices  32.2 us (7%)
  between operations  28.6 us (6%)
  matrix products  23.7 us (5%)
  other arithmetic  15.2 us (3%)
  local copies, waits for them, and re-layouts  14.1 us (3%)
    psum x4, blocking collectives, paired_sums(): lax.psum((jnp.sum(residual * residual), jnp.sum(residual * image)), ('gx'...  167 us
    psum x1, waiting for transfers between devices, one_after_other(): return lax.psum(half, other)  68.8 us
    psum x1, blocking collectives, one_after_other(): return lax.psum(half, other)  37.1 us
    ppermute x14, waiting for transfers between devices, with_halo(): before = lax.ppermute(last, axis, up)  24.5 us
    ppermute x14, starting transfers between devices, with_halo(): before = lax.ppermute(last, axis, up)  17.8 us
    dot_general x27, matrix products, grads_from_padded_deltas(): lax.dot_general(shifted, flat_inputs, (((1,), (1,)), ((), ())), preferred...  14.4 us
    ppermute x14, starting transfers between devices, with_halo(): after = lax.ppermute(leading, axis, down)  14.4 us
    ppermute x14, waiting for transfers between devices, with_halo(): after = lax.ppermute(leading, axis, down)  13.3 us
  transfers between devices with their start and end apart: 30, of which 24 were waited for; matrix products, arithmetic and copies ran while one was open for 4% of the time, Pallas kernels for 0%

profile of v1, /device:TPU:8, one launch (start us, length us, event | category | flops | bytes accessed | tf_op | source)
XLA Modules:
  0.0 437.2 jit_solution(4897420195304831478)
XLA Ops:
  8.0 1.5 collective-permute-start
  9.5 1.4 collective-permute-start.1
  10.9 1.6 collective-permute-done
  13.1 0.8 pad_maximum_fusion.50
  14.5 1.0 collective-permute-done.3
  15.5 2.0 collective-permute-done.2
  17.5 0.9 fusion.98
  18.5 2.5 collective-permute-start.4
  21.4 1.6 collective-permute-done.4
  23.0 1.5 collective-permute-done.5
  24.6 1.7 collective-permute-start.7
  26.3 1.4 collective-permute-done.6
  28.4 42.3 %all-reduce.3 = (f32[]{:T(128)}, f32[]{:T(128)}) all-reduce(f32[]{:T(128)} %get-tuple-element.25, f32[]{:T(128)} %get-tuple-element.24), channel_id=1, replica_groups=mesh['gx'=8,'gy'=4] {'gx','gy'}, use_global_device_ids=true, to_apply=%region_1.0 | all-reduce | flops 2 | bytes 16 | tf_op jit(solution)/shard_map/psum | solution.py:51
  72.1 2.5 collective-permute-start.8
  75.0 1.6 collective-permute-done.8
  76.6 1.6 collective-permute-done.9
  78.3 1.7 collective-permute-start.11
  80.0 1.4 collective-permute-done.10
  82.1 41.4 %all-reduce.2 = (f32[]{:T(128)}, f32[]{:T(128)}) all-reduce(f32[]{:T(128)} %get-tuple-element.23, f32[]{:T(128)} %get-tuple-element.22), channel_id=1, replica_groups=mesh['gx'=8,'gy'=4] {'gx','gy'}, use_global_device_ids=true, to_apply=%region_5.0 | all-reduce | flops 2 | bytes 16 | tf_op jit(solution)/shard_map/psum | solution.py:51
  128.3 2.5 collective-permute-start.12
  131.2 1.6 collective-permute-done.12
  132.8 1.6 collective-permute-done.13
  134.4 1.7 collective-permute-start.15
  136.2 1.4 collective-permute-done.14
  138.3 41.7 %all-reduce.1 = (f32[]{:T(128)}, f32[]{:T(128)}) all-reduce(f32[]{:T(128)} %get-tuple-element.21, f32[]{:T(128)} %get-tuple-element.20), channel_id=1, replica_groups=mesh['gx'=8,'gy'=4] {'gx','gy'}, use_global_device_ids=true, to_apply=%region_9.0 | all-reduce | flops 2 | bytes 16 | tf_op jit(solution)/shard_map/psum | solution.py:51
  184.1 2.5 collective-permute-start.16
  187.1 1.6 collective-permute-done.16
  188.6 1.6 collective-permute-done.17
  190.3 1.7 collective-permute-start.19
  192.0 0.9 pad_maximum_fusion.8
  194.1 41.4 %all-reduce = (f32[]{:T(128)}, f32[]{:T(128)}) all-reduce(f32[]{:T(128)} %get-tuple-element.19, f32[]{:T(128)} %get-tuple-element.18), channel_id=1, replica_groups=mesh['gx'=8,'gy'=4] {'gx','gy'}, use_global_device_ids=true, to_apply=%region_13.0 | all-reduce | flops 2 | bytes 16 | tf_op jit(solution)/shard_map/psum | solution.py:51
  244.7 1.4 convert_reduce_fusion
  249.2 2.5 collective-permute-start.20
  252.6 1.6 collective-permute-done.20
  254.2 1.6 collective-permute-done.21
  256.0 1.7 collective-permute-start.22
  258.1 5.7 %collective-permute-done.23 = bf16[64,18,1]{2,0,1:T(8,128)(2,1)S(1)} collective-permute-done((bf16[64,18,1]{2,0,1:T(8,128)(2,1)S(1)}, bf16[64,18,1]{2,0,1:T(8,128)(2,1)S(1)}, u32[]{:S(2)}, u32[]{:S(2)}) %collective-permute-start.23) | collective-permute-done | bytes 2336 | tf_op jit(solution)/shard_map/ppermute | solution.py:23
  264.0 0.8 maximum_maximum_fusion
  264.8 0.9 fusion.28
  265.8 1.2 slice_bitcast_fusion.6
  266.9 0.8 fusion.21
  267.8 0.8 fusion.27
  268.6 0.9 fusion.26
  269.6 0.8 fusion.25
  270.4 0.8 fusion.24
  271.3 0.9 fusion.23
  277.3 1.2 convert_reduce_fusion.1
  278.6 2.7 collective-permute-start.24
  281.8 0.8 fusion.20
  282.6 0.8 fusion.22
  284.2 1.0 copy.80
  286.1 1.3 collective-permute-start.26
  287.5 1.0 copy.83
  288.5 1.0 copy.77
  289.5 2.7 collective-permute-done.27
  292.2 3.4 collective-permute-done.26
  295.6 0.8 maximum_maximum_fusion.1
  296.4 0.8 slice_bitcast_fusion.1
  297.6 1.6 slice_bitcast_fusion
  302.0 12.8 %all-reduce.5 = (f32[9,64,2]{1,2,0:T(2,128)S(1)}, f32[9,2,64]{2,1,0:T(2,128)S(1)}, f32[64]{0:T(128)S(1)}, f32[64]{0:T(128)S(1)}) all-reduce(f32[9,64,2]{1,2,0:T(2,128)S(1)} %fusion.40, f32[9,2,64]{2,1,0:T(2,128)S(1)} %fusion.31, f32[64]{0:T(128)S(1)} %get-tuple-element.44, ...), channel_id=1, replica_groups=mesh['gx'=8,'gy'=4] {'gy'}, use_global_device_ids=true, to_apply=%region_16.0 | all-reduce | flops 2432 | bytes 19456 | tf_op jit(solution)/shard_map/psum | solution.py:12
  314.8 37.1 %all-reduce.4 = (f32[9,64,2]{1,2,0:T(2,128)S(1)}, f32[9,2,64]{2,1,0:T(2,128)S(1)}, f32[64]{0:T(128)S(1)}, f32[64]{0:T(128)S(1)}) all-reduce(f32[9,64,2]{1,2,0:T(2,128)S(1)} %get-tuple-element.38, f32[9,2,64]{2,1,0:T(2,128)S(1)} %get-tuple-element.39, f32[64]{0:T(128)S(1)} %get-tuple-element.40, ...), channel_id=1, replica_groups=mesh['gx'=8,'gy'=4] {'gx'}, use_global_device_ids=true, to_apply=%region_17.0 | all-reduce | flops 2432 | bytes 19456 | tf_op jit(solution)/shard_map/psum | solution.py:13
  353.2 1.3 copy.84
  359.9 68.8 %all-reduce.11.cloned.1.call-done = f32[9,64,64]{2,1,0:T(8,128)} async-done(((f32[9,64,64]{2,1,0:T(8,128)}), f32[9,64,64]{2,1,0:T(8,128)}) %all-reduce.11.cloned.1.call-update) | async-done | bytes 147472 | tf_op jit(solution)/shard_map/psum | solution.py:13
  428.7 1.7 broadcast_multiply_fusion
  (145 shorter events, 34.4 us)
Async XLA Ops:
  7.2 290.1 %copy-start = (bf16[2,16,384]{2,1,0:T(8,128)(2,1)S(1)}, bf16[2,16,384]{2,1,0:T(8,128)(2,1)}, u32[]{:S(2)}) copy-start(bf16[2,16,384]{2,1,0:T(8,128)(2,1)} %param.8) | copy-start | bytes 73732
  7.2 233.1 %copy-start.11 = (bf16[9,2,64]{2,1,0:T(2,128)(2,1)S(1)}, bf16[9,2,64]{2,1,0:T(2,128)(2,1)}, u32[]{:S(2)}) copy-start(bf16[9,2,64]{2,1,0:T(2,128)(2,1)} %param.13) | copy-start | bytes 6916
  7.2 352.1 %all-reduce.9.cloned.1.call-start = ((), (), s32[]{:S(2)}) async-start(), calls=%async_computation | async-start | bytes 589824 | tf_op jit(solution)/shard_map/psum | solution.py:12
  8.0 4.5 %collective-permute-start = (f32[2,1,384]{2,1,0:T(1,128)S(1)}, f32[2,1,384]{2,1,0:T(1,128)S(1)}, u32[]{:S(2)}, u32[]{:S(2)}) collective-permute-start(f32[2,1,384]{2,1,0:T(1,128)S(1)} %get-tuple-element.82), channel_id=1, source_target_pairs={{0,4},{4,8},{8,12},{12,16},{16,20},{20,24},{24,28},{28,0},{1,5},{5... | collective-permute-start | bytes 9224 | tf_op jit(solution)/shard_map/ppermute | solution.py:23
  9.5 3.6 collective-permute-start.1
  13.9 1.6 collective-permute-start.3
  14.0 3.5 collective-permute-start.2
  18.5 4.5 %collective-permute-start.4 = (f32[2,384]{1,0:T(2,128)S(1)}, f32[2,384]{1,0:T(2,128)S(1)}, u32[]{:S(2)}, u32[]{:S(2)}) collective-permute-start(f32[2,384]{1,0:T(2,128)S(1)} %get-tuple-element.107), channel_id=1, source_target_pairs={{0,4},{4,8},{8,12},{12,16},{16,20},{20,24},{24,28},{28,0},{1,5},{5... | collective-permute-start | bytes 9224 | tf_op jit(solution)/shard_map/ppermute | solution.py:23
  20.9 3.6 collective-permute-start.5
  24.6 3.1 collective-permute-start.6
  24.6 3.1 collective-permute-start.7
  72.1 4.5 %collective-permute-start.8 = (f32[2,384]{1,0:T(2,128)S(1)}, f32[2,384]{1,0:T(2,128)S(1)}, u32[]{:S(2)}, u32[]{:S(2)}) collective-permute-start(f32[2,384]{1,0:T(2,128)S(1)} %get-tuple-element.105), channel_id=1, source_target_pairs={{0,4},{4,8},{8,12},{12,16},{16,20},{20,24},{24,28},{28,0},{1,5},{5... | collective-permute-start | bytes 9224 | tf_op jit(solution)/shard_map/ppermute | solution.py:23
  74.6 3.6 collective-permute-start.9
  78.3 3.1 collective-permute-start.10
  78.3 3.1 collective-permute-start.11
  128.3 4.5 %collective-permute-start.12 = (f32[2,384]{1,0:T(2,128)S(1)}, f32[2,384]{1,0:T(2,128)S(1)}, u32[]{:S(2)}, u32[]{:S(2)}) collective-permute-start(f32[2,384]{1,0:T(2,128)S(1)} %get-tuple-element.103), channel_id=1, source_target_pairs={{0,4},{4,8},{8,12},{12,16},{16,20},{20,24},{24,28},{28,0},{1,5},{5... | collective-permute-start | bytes 9224 | tf_op jit(solution)/shard_map/ppermute | solution.py:23
  130.8 3.6 collective-permute-start.13
  134.4 3.1 collective-permute-start.14
  134.4 3.1 collective-permute-start.15
  184.1 4.5 %collective-permute-start.16 = (f32[2,384]{1,0:T(2,128)S(1)}, f32[2,384]{1,0:T(2,128)S(1)}, u32[]{:S(2)}, u32[]{:S(2)}) collective-permute-start(f32[2,384]{1,0:T(2,128)S(1)} %get-tuple-element.101), channel_id=1, source_target_pairs={{0,4},{4,8},{8,12},{12,16},{16,20},{20,24},{24,28},{28,0},{1,5},{5... | collective-permute-start | bytes 9224 | tf_op jit(solution)/shard_map/ppermute | solution.py:23
  186.6 3.6 collective-permute-start.17
  190.3 3.1 collective-permute-start.18
  190.3 3.1 collective-permute-start.19
  243.6 1.1 copy-start.6
  249.2 5.0 %collective-permute-start.20 = (bf16[64,1,384]{2,0,1:T(8,128)(2,1)S(1)}, bf16[64,1,384]{2,0,1:T(8,128)(2,1)S(1)}, u32[]{:S(2)}, u32[]{:S(2)}) collective-permute-start(bf16[64,1,384]{2,0,1:T(8,128)(2,1)S(1)} %get-tuple-element.76), channel_id=1, source_target_pairs={{0,4},{4,8},{8,12},{12,16},{16,20},{20,24},{24,28},{28,0},{1,5},{5... | collective-permute-start | bytes 147464 | tf_op jit(solution)/shard_map/ppermute | solution.py:23
  251.7 4.1 collective-permute-start.21
  256.0 7.8 %collective-permute-start.23 = (bf16[64,18,1]{2,0,1:T(8,128)(2,1)S(1)}, bf16[64,18,1]{2,0,1:T(8,128)(2,1)S(1)}, u32[]{:S(2)}, u32[]{:S(2)}) collective-permute-start(bf16[64,18,1]{2,0,1:T(8,128)(2,1)S(1)} %get-tuple-element.67), channel_id=1, source_target_pairs={{0,1},{1,2},{2,3},{3,0},{4,5},{5,6},{6,7},{7,4},{8,9},{9,10},{10,1... | collective-permute-start | bytes 6920 | tf_op jit(solution)/shard_map/ppermute | solution.py:23
  256.0 8.0 %collective-permute-start.22 = (bf16[64,18,1]{2,0,1:T(8,128)(2,1)S(1)}, bf16[64,18,1]{2,0,1:T(8,128)(2,1)S(1)}, u32[]{:S(2)}, u32[]{:S(2)}) collective-permute-start(bf16[64,18,1]{2,0,1:T(8,128)(2,1)S(1)} %get-tuple-element.68), channel_id=1, source_target_pairs={{1,0},{2,1},{3,2},{0,3},{5,4},{6,5},{7,6},{4,7},{9,8},{10,9},{11,1... | collective-permute-start | bytes 6920 | tf_op jit(solution)/shard_map/ppermute | solution.py:24
  258.1 6.7 %copy-start.7 = (bf16[64,16,384]{2,1,0:T(8,128)(2,1)S(1)}, bf16[64,16,384]{2,1,0:T(8,128)(2,1)}, u32[]{:S(2)}) copy-start(bf16[64,16,384]{2,1,0:T(8,128)(2,1)} %param.9) | copy-start | bytes 2359300
  272.6 0.9 copy-start.9
  278.6 6.7 %collective-permute-start.24 = (bf16[64,1,384]{2,0,1:T(8,128)(2,1)S(1)}, bf16[64,1,384]{2,0,1:T(8,128)(2,1)S(1)}, u32[]{:S(2)}, u32[]{:S(2)}) collective-permute-start(bf16[64,1,384]{2,0,1:T(8,128)(2,1)S(1)} %get-tuple-element.72), channel_id=1, source_target_pairs={{0,4},{4,8},{8,12},{12,16},{16,20},{20,24},{24,28},{28,0},{1,5},{5... | collective-permute-start | bytes 147464 | tf_op jit(solution)/shard_map/ppermute | solution.py:23
  281.3 4.2 collective-permute-start.25
  283.4 0.7 copy-start.8
  284.2 144.5 %all-reduce.11.cloned.1.call-start = ((), (), s32[]{:S(2)}) async-start(), calls=%async_computation.1 | async-start | bytes 589824 | tf_op jit(solution)/shard_map/psum | solution.py:13
  285.6 6.6 %collective-permute-start.27 = (bf16[64,18,1]{2,0,1:T(8,128)(2,1)S(1)}, bf16[64,18,1]{2,0,1:T(8,128)(2,1)S(1)}, u32[]{:S(2)}, u32[]{:S(2)}) collective-permute-start(bf16[64,18,1]{2,0,1:T(8,128)(2,1)S(1)} %get-tuple-element.63), channel_id=1, source_target_pairs={{0,1},{1,2},{2,3},{3,0},{4,5},{5,6},{6,7},{7,4},{8,9},{9,10},{10,1... | collective-permute-start | bytes 6920 | tf_op jit(solution)/shard_map/ppermute | solution.py:23
  286.1 9.6 %collective-permute-start.26 = (bf16[64,18,1]{2,0,1:T(8,128)(2,1)S(1)}, bf16[64,18,1]{2,0,1:T(8,128)(2,1)S(1)}, u32[]{:S(2)}, u32[]{:S(2)}) collective-permute-start(bf16[64,18,1]{2,0,1:T(8,128)(2,1)S(1)} %get-tuple-element.64), channel_id=1, source_target_pairs={{1,0},{2,1},{3,2},{0,3},{5,4},{6,5},{7,6},{4,7},{9,8},{10,9},{11,1... | collective-permute-start | bytes 6920 | tf_op jit(solution)/shard_map/ppermute | solution.py:24
  301.7 52.8 %copy-start.2 = (bf16[16,8,8,384]{3,2,1,0:T(8,128)(2,1)S(1)}, bf16[16,8,8,384]{3,2,1,0:T(8,128)(2,1)}, u32[]{:S(2)}) copy-start(bf16[16,8,8,384]{3,2,1,0:T(8,128)(2,1)} %get-tuple-element.50) | copy-start | bytes 2359300
  353.2 1.4 copy-start.1
  354.8 0.7 copy-start.10
  354.9 1.1 copy-start.5
  355.5 1.2 copy-start.3
  356.4 1.2 copy-start.4
Sparse Core Ops, SparseCore 0:
  284.3 35.1 all-reduce.8
  359.5 69.1 all-reduce.10
